TPU v7x, 32 devices: a whole 2x2x4 slice. The times are simulated.
32 devices in a mesh: pb: 8 (over y, x, core), kv: 4 (over z).
Axes of the slice: x: 2, y: 2, z: 4, core: 2. Of those that a mesh axis runs over, the one named last changes fastest.
Arguments:
- queries: bfloat16 [4096, 1024], P(('pb', 'kv')), may hold values from -6 to 6
- key_rows: bfloat16 [4096, 128], P(('kv', 'pb')), may hold values from -6 to 6
- value_rows: bfloat16 [4096, 128], P(('kv', 'pb')), may hold values from -0.59765625 to 0.59765625
- output: bfloat16 [4096, 1024], P(('pb', 'kv')), may hold values from -1.796875 to 1.796875
- out_grad: bfloat16 [4096, 1024], P(('pb', 'kv')), may hold values from -6 to 6
- log_norm: float32 [8, 4096], P(None, ('pb', 'kv')), as said below
- positions: int32 [4096], replicated, may hold values from 0 to 4095, as said below
Outputs:
- query_grad: float32 [4096, 1024], P(('pb', 'kv'))
- key_grad: float32 [4096, 128], P(('kv', 'pb'))
- value_grad: float32 [4096, 128], P(('kv', 'pb'))
Inputs may be any that keep to these rules, and one draw needn't show every extreme that they name: A permutation of 0 to 4095: row r holds the token at position positions[r]. log_norm[h, r] - log(1 + positions[r]) lies between 0.25 and 0.75.
All inputs are finite; a program needn't handle non-finite values.
Results may differ from a plain program's by a relative error of at most 0.0041.
Values may be sent and summed in bfloat16 or wider, within the bound.
A program may use at most 64 MiB of HBM per device.

v0:
```python
import functools
import math

import jax
import jax.numpy as jnp
from jax import lax
from jax.experimental import pallas as pl
from jax.experimental.pallas import tpu as pltpu
from jax.sharding import PartitionSpec as P

MESH = pl.DeviceIdType.MESH
LOG2E = math.log2(math.e)
HIDDEN = -1e30
GROUPED = 4


def flip(index, mask, count):
    total, bit = 0, 1
    while bit < count:
        digit = (index // bit) % 2
        total = total + bit * ((1 - digit) if mask & bit else digit)
        bit *= 2
    return total


def kernel(
    planes, layers, q_ref, k_ref, v_ref, o_ref, g_ref, n_ref, pos_ref,
    dq_ref, dkv_ref,
    q_all, g_all, o_own, kv_own, n_own, pos, kv_all, norm, delta, bias, dkv_acc, dq_acc, dq_in,
    own, out1, in1, out2, in2,
    load, pair_send, pair_recv, z_send, z_recv, p_send, p_recv, r1_send, r1_recv, r2_send, r2_recv,
):
    pb, z = lax.axis_index("pb"), lax.axis_index("kv")
    p, core = pb // 2, pb % 2
    rows, heads = q_ref.shape[0], n_ref.shape[0]
    keys, width = k_ref.shape
    part_rows = keys // 2
    inv_root = 1.0 / math.sqrt(width)

    loads = [
        pltpu.make_async_copy(src, dst, load.at[i])
        for i, (src, dst) in enumerate((
            (k_ref, kv_own.at[0]), (v_ref, kv_own.at[1]),
            (q_ref, q_all.at[pl.ds(0, rows)]), (g_ref, g_all.at[pl.ds(0, rows)]),
            (o_ref, o_own), (n_ref, n_own), (pos_ref, pos),
        ))
    ]
    for copy in loads:
        copy.start()

    partner = {"pb": p * 2 + 1 - core, "kv": z}
    z_peers = [(z + step) % layers for step in range(layers)]
    p_peers = [flip(p, step, planes) for step in range(planes)]

    def above(step):
        return {"pb": pb, "kv": z_peers[step]}

    def beside(step):
        return {"pb": p_peers[step] * 2 + core, "kv": z}

    def remote(src, dst, send, recv, device):
        return pltpu.make_async_remote_copy(
            src_ref=src, dst_ref=dst, send_sem=send, recv_sem=recv,
            device_id=device, device_id_type=MESH,
        )

    peers = [partner] + [above(s) for s in range(1, layers)] + [beside(s) for s in range(1, planes)]
    barrier = pltpu.get_barrier_semaphore()
    for peer in peers:
        pl.semaphore_signal(barrier, inc=1, device_id=peer, device_id_type=MESH)
    pl.semaphore_wait(barrier, len(peers))

    def place_of(layer):
        return pl.ds(pl.multiple_of(layer * part_rows, part_rows), part_rows)

    def own_part(half):
        return kv_own.at[:, pl.ds(half * part_rows, part_rows)]

    sent = []

    def start(copy):
        copy.start()
        sent.append(copy)
        return copy

    loads[0].wait()
    loads[1].wait()
    z_copies, p_copies = {}, {}
    for half in range(2):
        for step in range(1, layers):
            z_copies[half, step] = start(remote(
                own_part(half), kv_all.at[p, half, :, place_of(z)],
                z_send.at[half, step - 1], z_recv.at[half, step - 1], above(step),
            ))

    def spread(half, step_z, step):
        place = place_of((z + layers - step_z) % layers)
        landed = kv_all.at[p, half, :, place]
        p_copies[half, step_z, step] = start(remote(
            own_part(half) if step_z == 0 else landed, landed,
            p_send.at[half, step_z, step - 1], p_recv.at[half, step_z, step - 1], beside(step),
        ))

    relayed, waited = planes == 4, set()
    near = [step for step in range(1, planes) if step & (step - 1) == 0]
    far = [step for step in range(1, planes) if step & (step - 1)]
    for step in near:
        spread(0, 0, step)

    loads[2].wait()
    loads[3].wait()
    second = pl.ds(rows, rows)
    pair_copies = [
        start(remote(full.at[pl.ds(0, rows)], full.at[second], pair_send.at[i], pair_recv.at[i], partner))
        for i, full in enumerate((q_all, g_all))
    ]

    for copy in loads[4:]:
        copy.wait()
    norm[:, :rows] = n_own[...] * LOG2E
    for h in range(heads):
        part = slice(h * width, (h + 1) * width)
        product = g_all[:rows, part].astype(jnp.float32) * o_own[:, part].astype(jnp.float32)
        delta[h : h + 1, :rows] = jnp.sum(product.T, axis=0, keepdims=True)
    for i, stat in enumerate((norm, delta)):
        pair_copies.append(start(remote(
            stat.at[:, pl.ds(0, rows)], stat.at[:, second], pair_send.at[2 + i], pair_recv.at[2 + i], partner
        )))
    for half in range(2):
        kv_all[p, half, :, place_of(z)] = kv_own[:, half * part_rows : (half + 1) * part_rows]

    pos_own = pos[pl.ds(pb * layers + z, 1), :]
    pos_partner = pos[pl.ds((p * 2 + 1 - core) * layers + z, 1), :]

    def make_bias(column, carry):
        for layer in range(layers):
            row = pos[pl.ds(layer * (2 * planes) + column * 2 + core, 1), :]
            key_pos = jnp.broadcast_to(row, (rows, keys)).T
            place = slice(layer * part_rows, (layer + 1) * part_rows)
            for side, query_pos in enumerate((pos_own, pos_partner)):
                block = jnp.where(key_pos <= query_pos, 0.0, HIDDEN)
                for half in range(2):
                    bias[column, half, place, side * rows : (side + 1) * rows] = block[
                        half * part_rows : (half + 1) * part_rows
                    ]
        return carry

    def gather(half):
        for step_z in range(1, layers):
            z_copies[half, step_z].wait_recv()
            for step in near:
                spread(half, step_z, step)
        if relayed:
            return
        for step in far:
            for step_z in range(layers):
                spread(half, step_z, step)

    def relay(half):
        for i, source in enumerate(near):
            target = near[1 - i]
            for step_z in range(i * layers // 2, (i + 1) * layers // 2):
                p_copies[half, step_z, source].wait_recv()
                landed = kv_all.at[p_peers[source], half, :, place_of((z + layers - step_z) % layers)]
                p_copies[half, step_z, far[0]] = start(remote(
                    landed, landed,
                    p_send.at[half, step_z, far[0] - 1], p_recv.at[half, step_z, far[0] - 1], beside(target),
                ))
                waited.add((half, step_z, source))

    gather(0)
    for step in near:
        spread(1, 0, step)
    lax.fori_loop(0, planes, make_bias, 0)
    for copy in pair_copies:
        copy.wait_recv()

    last = (((1,), (1,)), ((), ()))

    def compute(column, half, first):
        keys_turned = kv_all[column, half, 0].T

        def one_head(h):
            part = pl.ds(pl.multiple_of(h * width, width), width)
            q, g = q_all[:, part], g_all[:, part]
            scores = lax.dot_general(kv_all[column, half, 0], q, last, preferred_element_type=jnp.float32)
            grad_probs = lax.dot_general(kv_all[column, half, 1], g, last, preferred_element_type=jnp.float32)
            probs = jnp.exp2(scores * (inv_root * LOG2E) - norm[pl.ds(h, 1), :] + bias[column, half])
            probs_low = probs.astype(jnp.bfloat16)
            grad_scores = (probs * (grad_probs - delta[pl.ds(h, 1), :]) * inv_root).astype(jnp.bfloat16)
            dv = jnp.dot(probs_low, g, preferred_element_type=jnp.float32)
            dk = jnp.dot(grad_scores, q, preferred_element_type=jnp.float32)
            dq = jnp.dot(keys_turned, grad_scores, preferred_element_type=jnp.float32)
            return dk, dv, dq

        dkv_acc[...] = jnp.zeros_like(dkv_acc)

        def body(i, carry):
            results = [one_head(GROUPED * i + j) for j in range(GROUPED)]
            for side in range(2):
                dkv_acc[side] += sum(result[side] for result in results)
            for j in range(GROUPED):
                dq = results[j][2]
                for side in range(2):
                    piece = dq[:, side * rows : (side + 1) * rows]
                    if first:
                        dq_acc[side, GROUPED * i + j] = piece
                    else:
                        dq_acc[side, GROUPED * i + j] += piece
            return carry

        lax.fori_loop(0, heads // GROUPED, body, 0)

    r1_copies, r2_copies = {}, {}

    def compute_peer(half, step):
        for step_z in range(layers):
            if (half, step_z, step) not in waited:
                p_copies[half, step_z, step].wait_recv()
        compute(p_peers[step], half, False)
        out1[half, step - 1] = dkv_acc[...].astype(jnp.bfloat16)
        r1_copies[half, step] = start(remote(
            out1.at[half, step - 1], in1.at[half, step - 1],
            r1_send.at[half, step - 1], r1_recv.at[half, step - 1], beside(step),
        ))

    def compute_own(half, first):
        compute(p, half, first)
        own[half] = dkv_acc[...]

    def plane_sum(half, layer):
        place = place_of(layer)
        total = own[half, :, place]
        for step in range(1, planes):
            total = total + in1[half, step - 1, :, place].astype(jnp.float32)
        return total

    def reduce_plane(half):
        for step in range(1, planes):
            r1_copies[half, step].wait_recv()
        for step in range(1, layers):
            out2[half, step - 1] = plane_sum(half, z_peers[step]).astype(jnp.bfloat16)
            r2_copies[half, step] = start(remote(
                out2.at[half, step - 1], in2.at[half, step - 1],
                r2_send.at[half, step - 1], r2_recv.at[half, step - 1], above(step),
            ))

    compute_own(0, True)
    gather(1)
    if relayed:
        relay(0)
    order = near + far
    for step in order:
        compute_peer(0, step)
        if relayed and step == near[-1]:
            relay(1)
    for step in order:
        compute_peer(1, step)
        if step == order[-2]:
            reduce_plane(0)
    compute_own(1, False)
    back = start(remote(dq_acc.at[1], dq_in, pair_send.at[4], pair_recv.at[4], partner))
    reduce_plane(1)

    back.wait_recv()
    for h in range(heads):
        part = slice(h * width, (h + 1) * width)
        dq_ref[:, part] = (dq_acc[0, h] + dq_in[h]).T

    for half in range(2):
        total = plane_sum(half, z)
        for step in range(1, layers):
            r2_copies[half, step].wait_recv()
            total = total + in2[half, step - 1].astype(jnp.float32)
        dkv_ref[:, half * part_rows : (half + 1) * part_rows] = total
    for copy in sent:
        copy.wait_send()


def finish(dq_in, dkv_in, dq_ref, dk_ref, dv_ref):
    dq_ref[...] = dq_in[...]
    dk_ref[...] = dkv_in[0]
    dv_ref[...] = dkv_in[1]


def solution(mesh):
    planes, layers = mesh.shape["pb"] // 2, mesh.shape["kv"]

    def step(queries, key_rows, value_rows, output, out_grad, log_norm, positions):
        rows, columns = queries.shape
        keys, width = key_rows.shape
        heads = log_norm.shape[0]
        part_rows = keys // 2
        column = layers * part_rows
        low, full = jnp.bfloat16, jnp.float32
        vmem, hbm = pl.BlockSpec(memory_space=pltpu.VMEM), pl.BlockSpec(memory_space=pl.ANY)
        dma = pltpu.SemaphoreType.DMA
        pos = positions.reshape(-1, rows)
        dq, dkv = pl.pallas_call(
            functools.partial(kernel, planes, layers),
            out_shape=(
                jax.ShapeDtypeStruct((rows, columns), full),
                jax.ShapeDtypeStruct((2, keys, width), full),
            ),
            in_specs=[hbm] * 7,
            out_specs=(vmem, vmem),
            scratch_shapes=[
                pltpu.VMEM((2 * rows, columns), low),
                pltpu.VMEM((2 * rows, columns), low),
                pltpu.VMEM((rows, columns), low),
                pltpu.VMEM((2, keys, width), low),
                pltpu.VMEM(log_norm.shape, full),
                pltpu.VMEM(pos.shape, jnp.int32),
                pltpu.VMEM((planes, 2, 2, column, width), low),
                pltpu.VMEM((heads, 2 * rows), full),
                pltpu.VMEM((heads, 2 * rows), full),
                pltpu.VMEM((planes, 2, column, 2 * rows), full),
                pltpu.VMEM((2, column, width), full),
                pltpu.VMEM((2, heads, width, rows), full),
                pltpu.VMEM((heads, width, rows), full),
                pltpu.VMEM((2, 2, column, width), full),
                pltpu.VMEM((2, planes - 1, 2, column, width), low),
                pltpu.VMEM((2, planes - 1, 2, column, width), low),
                pltpu.VMEM((2, layers - 1, 2, part_rows, width), low),
                pltpu.VMEM((2, layers - 1, 2, part_rows, width), low),
                dma((7,)), dma((5,)), dma((5,)),
                dma((2, layers - 1)), dma((2, layers - 1)),
                dma((2, layers, planes - 1)), dma((2, layers, planes - 1)),
                dma((2, planes - 1)), dma((2, planes - 1)),
                dma((2, layers - 1)), dma((2, layers - 1)),
            ],
            compiler_params=pltpu.CompilerParams(
                collective_id=0, has_side_effects=True, vmem_limit_bytes=58 * 2**20
            ),
        )(queries, key_rows, value_rows, output, out_grad, log_norm, pos)
        return pl.pallas_call(
            finish,
            out_shape=(
                jax.ShapeDtypeStruct((rows, columns), full),
                jax.ShapeDtypeStruct((keys, width), full),
                jax.ShapeDtypeStruct((keys, width), full),
            ),
            in_specs=[vmem] * 2,
            out_specs=(vmem, vmem, vmem),
        )(dq, dkv)

    return jax.shard_map(
        step,
        mesh=mesh,
        in_specs=(
            P(("pb", "kv"), None),
            P(("kv", "pb"), None),
            P(("kv", "pb"), None),
            P(("pb", "kv"), None),
            P(("pb", "kv"), None),
            P(None, ("pb", "kv")),
            P(),
        ),
        out_specs=(P(("pb", "kv"), None), P(("kv", "pb"), None), P(("kv", "pb"), None)),
        check_vma=False,
    )
```

profile of v0, /device:TPU:0, one launch (start us, length us, event | category | flops | bytes accessed | tf_op | source)
XLA Modules:
  0.0 42.8 jit_solution(17604500099857684376)
XLA Ops:
  0.6 40.3 %shard_map.94 = (f32[128,1024]{1,0:T(8,128)}, f32[2,128,128]{2,1,0:T(8,128)}) custom-call(bf16[128,1024]{1,0:T(8,128)(2,1)} %q_ref.1, bf16[128,128]{1,0:T(8,128)(2,1)} %k_ref.1, bf16[128,128]{1,0:T(8,128)(2,1)} %v_ref.1, bf16[128,1024]{1,0:T(8,128)(2,1)} %o_ref.1, bf16[128,1024]{1,0:T(8,128)(2,1)} %g_ref.1, f32[8,128]{1,0:T(8,128)} %n_ref.1, s32[32,128]{1,0:T(8,128)} %bitcast.1), custom_call_target="tpu_custom_call" | custom-call | tf_op jit(solution)/shard_map/pallas_call | solution.py:299
  40.9 1.9 %shard_map.95 = (f32[128,1024]{1,0:T(8,128)}, f32[128,128]{1,0:T(8,128)}, f32[128,128]{1,0:T(8,128)}) custom-call(f32[128,1024]{1,0:T(8,128)} %get-tuple-element.5.dq_in, f32[2,128,128]{2,1,0:T(8,128)} %get-tuple-element.6.dkv_in), custom_call_target="tpu_custom_call" | custom-call | tf_op jit(solution)/shard_map/pallas_call | solution.py:336
where the time goes:
time: 43 us; the launch traced here: 42.8 us
  Pallas kernels  42.2 us (98%)
  between operations  0.64 us (1%)
    pallas_call x1, Pallas kernels, step(): pl.pallas_call(functools.partial(kernel, planes, layers), out_shape=(jax....  40.3 us
    pallas_call x1, Pallas kernels, step(): pl.pallas_call(finish, out_shape=(jax.ShapeDtypeStruct((rows, columns), f...  1.9 us

commit v1 on v0

--- a/solution.py
+++ b/solution.py
@@ -12,6 +12,26 @@
 LOG2E = math.log2(math.e)
 HIDDEN = -1e30
 GROUPED = 4
+ALONG, UPWARD, STRAIGHT, RELAYED = range(4)
+START, PASS, COMPUTE, ADD = range(4)
+KEY_ROUTE = (
+    (),
+    (STRAIGHT, STRAIGHT, ALONG, ALONG),
+    (STRAIGHT, STRAIGHT, ALONG, ALONG),
+    (RELAYED, UPWARD, ALONG, UPWARD),
+)
+SUM_ROUTE = (
+    (),
+    (ALONG, STRAIGHT, ALONG, ALONG),
+    (ALONG, STRAIGHT, ALONG, ALONG),
+    (ALONG, UPWARD, ALONG, ALONG),
+)
+STEPS = (
+    (START, 2, 0), (START, 0, 2), (START, 1, 1), (START, 1, 0), (PASS, 2, 0), (START, 0, 3), (START, 2, 1),
+    (COMPUTE, (2, 0), (0, 0)), (PASS, 0, 2), (COMPUTE, (0, 2), (1, 0)), (PASS, 3, 0), (COMPUTE, (3, 0), (1, 1)),
+    (START, 0, 1), (PASS, 0, 3), (COMPUTE, (2, 1), (1, 2)), (COMPUTE, (2, 2), (3, 2)), (COMPUTE, (3, 1), (3, 3)),
+    (COMPUTE, (2, 3), (1, 3)), (ADD, 0, 2), (COMPUTE, (0, 1), (0, 3)), (ADD, 0, 1), (ADD, 0, 3), (ADD, 3, 0),
+)
 
 
 def flip(index, mask, count):
@@ -277,6 +297,212 @@
         copy.wait_send()
 
 
+def square(
+    planes, layers, q_ref, k_ref, v_ref, o_ref, g_ref, n_ref, pos_ref,
+    dq_ref, dkv_ref,
+    q_all, g_all, o_own, n_own, pos, kv_all, norm, delta, bias, dq_acc, dq_in,
+    own, out, into,
+    load, pair_send, pair_recv, k_send, k_recv, s_send, s_recv,
+):
+    pb, z = lax.axis_index("pb"), lax.axis_index("kv")
+    p, core = pb // 2, pb % 2
+    rows, heads = q_ref.shape[0], n_ref.shape[0]
+    keys, width = k_ref.shape
+    inv_root = 1.0 / math.sqrt(width)
+    low, full = jnp.bfloat16, jnp.float32
+    here = (0, 0)
+
+    loads = [
+        pltpu.make_async_copy(src, dst, load.at[i])
+        for i, (src, dst) in enumerate((
+            (k_ref, kv_all.at[0, 0, 0]), (v_ref, kv_all.at[0, 0, 1]),
+            (q_ref, q_all.at[pl.ds(0, rows)]), (g_ref, g_all.at[pl.ds(0, rows)]),
+            (o_ref, o_own), (n_ref, n_own), (pos_ref, pos),
+        ))
+    ]
+    for copy in loads:
+        copy.start()
+
+    partner = {"pb": p * 2 + 1 - core, "kv": z}
+    z_peers = [flip(z, j, layers) for j in range(layers)]
+    p_peers = [flip(p, c, planes) for c in range(planes)]
+
+    def at(c, j):
+        return {"pb": p_peers[c] * 2 + core, "kv": z_peers[j]}
+
+    sent = []
+
+    def send(src, dst, send_sem, recv_sem, device):
+        copy = pltpu.make_async_remote_copy(
+            src_ref=src, dst_ref=dst, send_sem=send_sem, recv_sem=recv_sem,
+            device_id=device, device_id_type=MESH,
+        )
+        copy.start()
+        sent.append(copy)
+        return copy
+
+    def across(j):
+        return 1 + j % 2
+
+    def sum_goes(c, j):
+        if c == 0:
+            return (0, j)
+        return {ALONG: (c, 0), UPWARD: (0, j), STRAIGHT: (c, j), RELAYED: (across(j), 0)}[SUM_ROUTE[c][j]]
+
+    def joins(c, j):
+        if c == 0:
+            return [(i, j) for i in range(1, planes) if SUM_ROUTE[i][j] == ALONG]
+        found = [(c, i) for i in range(1, layers) if j == 0 and SUM_ROUTE[c][i] == UPWARD]
+        if c == 3 - across(j) and SUM_ROUTE[3][j] == RELAYED:
+            found.append((3, j))
+        return found
+
+    def key_hops(c, j):
+        hops = []
+        if c == 0 and j:
+            hops += [(i, 0) for i in range(1, planes) if KEY_ROUTE[i][j] == ALONG]
+        if c and j == 0:
+            hops += [(0, i) for i in range(1, layers) if KEY_ROUTE[c][i] == UPWARD]
+        if c == 3 - across(j) and KEY_ROUTE[3][j] == RELAYED:
+            hops.append((3 - c, 0))
+        return hops
+
+    units = [(c, j) for c in range(planes) for j in range(layers)]
+    starts = [step[1:] for step in STEPS if step[0] == START]
+    peers = {*starts, *(hop for unit in units for hop in key_hops(*unit)), *(sum_goes(*unit) for unit in units)}
+    peers = [partner] + [at(*peer) for peer in sorted(peers - {here})]
+    barrier = pltpu.get_barrier_semaphore()
+    for peer in peers:
+        pl.semaphore_signal(barrier, inc=1, device_id=peer, device_id_type=MESH)
+    pl.semaphore_wait(barrier, len(peers))
+
+    coming = {}
+
+    def give(unit, hop):
+        c, j = unit[0] ^ hop[0], unit[1] ^ hop[1]
+        coming[c, j] = send(kv_all.at[unit], kv_all.at[c, j], k_send.at[c, j], k_recv.at[c, j], at(*hop))
+
+    def arrive(unit):
+        if unit in coming:
+            coming.pop(unit).wait_recv()
+
+    loads[0].wait()
+    loads[1].wait()
+    for unit in starts:
+        give(here, unit)
+
+    loads[2].wait()
+    loads[3].wait()
+    second = pl.ds(rows, rows)
+    pair_copies = [
+        send(ref.at[pl.ds(0, rows)], ref.at[second], pair_send.at[i], pair_recv.at[i], partner)
+        for i, ref in enumerate((q_all, g_all))
+    ]
+    for copy in loads[4:]:
+        copy.wait()
+    norm[:, :rows] = n_own[...] * LOG2E
+    for h in range(heads):
+        part = slice(h * width, (h + 1) * width)
+        product = g_all[:rows, part].astype(full) * o_own[:, part].astype(full)
+        delta[h : h + 1, :rows] = jnp.sum(product.T, axis=0, keepdims=True)
+    for i, stat in enumerate((norm, delta)):
+        pair_copies.append(send(
+            stat.at[:, pl.ds(0, rows)], stat.at[:, second], pair_send.at[2 + i], pair_recv.at[2 + i], partner
+        ))
+
+    pos_own = pos[pl.ds(pb * layers + z, 1), :]
+    pos_partner = pos[pl.ds((p * 2 + 1 - core) * layers + z, 1), :]
+    for c, j in units:
+        row = pos[pl.ds(z_peers[j] * (2 * planes) + p_peers[c] * 2 + core, 1), :]
+        key_pos = jnp.broadcast_to(row, (rows, keys)).T
+        for side, query_pos in enumerate((pos_own, pos_partner)):
+            bias[c, j, :, side * rows : (side + 1) * rows] = jnp.where(key_pos <= query_pos, 0.0, HIDDEN)
+    for copy in pair_copies:
+        copy.wait_recv()
+
+    last = (((1,), (1,)), ((), ()))
+
+    def compute(chunk, first):
+        def both(pick):
+            return jnp.concatenate([pick(c, j) for c, j in chunk], axis=0)
+
+        k = both(lambda c, j: kv_all[c, j, 0])
+        v = both(lambda c, j: kv_all[c, j, 1])
+        hidden = both(lambda c, j: bias[c, j])
+        turned = k.T
+        sums = None
+        for h in range(heads):
+            part = slice(h * width, (h + 1) * width)
+            q, g = q_all[:, part], g_all[:, part]
+            scores = lax.dot_general(k, q, last, preferred_element_type=full)
+            grad_probs = lax.dot_general(v, g, last, preferred_element_type=full)
+            probs = jnp.exp2(scores * (inv_root * LOG2E) - norm[h : h + 1, :] + hidden)
+            grad_scores = (probs * (grad_probs - delta[h : h + 1, :]) * inv_root).astype(low)
+            dv = jnp.dot(probs.astype(low), g, preferred_element_type=full)
+            dk = jnp.dot(grad_scores, q, preferred_element_type=full)
+            dq = jnp.dot(turned, grad_scores, preferred_element_type=full)
+            sums = (dk, dv) if sums is None else (sums[0] + dk, sums[1] + dv)
+            for side in range(2):
+                piece = dq[:, side * rows : (side + 1) * rows]
+                if first:
+                    dq_acc[side, h] = piece
+                else:
+                    dq_acc[side, h] += piece
+        for i, (c, j) in enumerate(chunk):
+            place = own if keeps(c, j) else out
+            for side, total in enumerate(sums):
+                place[c, j, side] = total[i * keys : (i + 1) * keys].astype(place.dtype)
+
+    def keeps(c, j):
+        return c == 0 or len(joins(c, j)) > 0
+
+    summed = {}
+
+    def total_of(unit, others):
+        total = own[unit]
+        for other in others:
+            summed[other].wait_recv()
+            total = total + into[other].astype(full)
+        return total
+
+    def ship(unit):
+        summed[unit] = send(out.at[unit], into.at[unit], s_send.at[unit], s_recv.at[unit], at(*sum_goes(*unit)))
+
+    first = True
+    for step in STEPS:
+        if step[0] == PASS:
+            unit = step[1:]
+            hops = key_hops(*unit)
+            if hops:
+                arrive(unit)
+            for hop in hops:
+                give(unit, hop)
+        elif step[0] == COMPUTE:
+            chunk = step[1:]
+            for unit in chunk:
+                arrive(unit)
+            compute(chunk, first)
+            first = False
+            for unit in chunk:
+                if not keeps(*unit):
+                    ship(unit)
+        elif step[0] == ADD:
+            unit = step[1:]
+            if keeps(*unit):
+                out[unit] = total_of(unit, joins(*unit)).astype(low)
+                ship(unit)
+
+    back = send(dq_acc.at[1], dq_in, pair_send.at[4], pair_recv.at[4], partner)
+    back.wait_recv()
+    for h in range(heads):
+        part = slice(h * width, (h + 1) * width)
+        dq_ref[:, part] = (dq_acc[0, h] + dq_in[h]).T
+    arrivals = [unit for unit in units if unit != here and (unit[0] == 0 or SUM_ROUTE[unit[0]][unit[1]] == STRAIGHT)]
+    dkv_ref[...] = total_of(here, arrivals + joins(*here))
+    for copy in sent:
+        copy.wait_send()
+
+
 def finish(dq_in, dkv_in, dq_ref, dk_ref, dv_ref):
     dq_ref[...] = dq_in[...]
     dk_ref[...] = dkv_in[0]
@@ -285,6 +511,7 @@
 
 def solution(mesh):
     planes, layers = mesh.shape["pb"] // 2, mesh.shape["kv"]
+    paired = planes == 4 and layers == len(KEY_ROUTE[1])
 
     def step(queries, key_rows, value_rows, output, out_grad, log_norm, positions):
         rows, columns = queries.shape
@@ -296,15 +523,30 @@
         vmem, hbm = pl.BlockSpec(memory_space=pltpu.VMEM), pl.BlockSpec(memory_space=pl.ANY)
         dma = pltpu.SemaphoreType.DMA
         pos = positions.reshape(-1, rows)
-        dq, dkv = pl.pallas_call(
-            functools.partial(kernel, planes, layers),
-            out_shape=(
-                jax.ShapeDtypeStruct((rows, columns), full),
-                jax.ShapeDtypeStruct((2, keys, width), full),
-            ),
-            in_specs=[hbm] * 7,
-            out_specs=(vmem, vmem),
-            scratch_shapes=[
+        if paired:
+            body = square
+            scratch = [
+                pltpu.VMEM((2 * rows, columns), low),
+                pltpu.VMEM((2 * rows, columns), low),
+                pltpu.VMEM((rows, columns), low),
+                pltpu.VMEM(log_norm.shape, full),
+                pltpu.VMEM(pos.shape, jnp.int32),
+                pltpu.VMEM((planes, layers, 2, keys, width), low),
+                pltpu.VMEM((heads, 2 * rows), full),
+                pltpu.VMEM((heads, 2 * rows), full),
+                pltpu.VMEM((planes, layers, keys, 2 * rows), full),
+                pltpu.VMEM((2, heads, width, rows), full),
+                pltpu.VMEM((heads, width, rows), full),
+                pltpu.VMEM((planes, layers, 2, keys, width), full),
+                pltpu.VMEM((planes, layers, 2, keys, width), low),
+                pltpu.VMEM((planes, layers, 2, keys, width), low),
+                dma((7,)), dma((5,)), dma((5,)),
+                dma((planes, layers)), dma((planes, layers)),
+                dma((planes, layers)), dma((planes, layers)),
+            ]
+        else:
+            body = kernel
+            scratch = [
                 pltpu.VMEM((2 * rows, columns), low),
                 pltpu.VMEM((2 * rows, columns), low),
                 pltpu.VMEM((rows, columns), low),
@@ -328,7 +570,16 @@
                 dma((2, layers, planes - 1)), dma((2, layers, planes - 1)),
                 dma((2, planes - 1)), dma((2, planes - 1)),
                 dma((2, layers - 1)), dma((2, layers - 1)),
-            ],
+            ]
+        dq, dkv = pl.pallas_call(
+            functools.partial(body, planes, layers),
+            out_shape=(
+                jax.ShapeDtypeStruct((rows, columns), full),
+                jax.ShapeDtypeStruct((2, keys, width), full),
+            ),
+            in_specs=[hbm] * 7,
+            out_specs=(vmem, vmem),
+            scratch_shapes=scratch,
             compiler_params=pltpu.CompilerParams(
                 collective_id=0, has_side_effects=True, vmem_limit_bytes=58 * 2**20
             ),

time: 43 us -> 36 us (0.84)
  Pallas kernels: 42.2 us -> 35.3 us
    pallas_call x1, Pallas kernels: 40.3 us -> 33.3 us  [step(): pl.pallas_call(functools.partial(body, planes, layers), out_shape=(jax.Sh...]
where the time goes in v1:
time: 36 us; the launch traced here: 35.9 us
  Pallas kernels  35.3 us (98%)
  between operations  0.64 us (2%)
    pallas_call x1, Pallas kernels, step(): pl.pallas_call(functools.partial(body, planes, layers), out_shape=(jax.Sh...  33.3 us
    pallas_call x1, Pallas kernels, step(): pl.pallas_call(finish, out_shape=(jax.ShapeDtypeStruct((rows, columns), f...  1.9 us

profile of v1, /device:TPU:0, one launch (start us, length us, event | category | flops | bytes accessed | tf_op | source)
XLA Modules:
  0.0 35.9 jit_solution(6368860374749792000)
XLA Ops:
  0.6 33.3 %shard_map.94 = (f32[128,1024]{1,0:T(8,128)}, f32[2,128,128]{2,1,0:T(8,128)}) custom-call(bf16[128,1024]{1,0:T(8,128)(2,1)} %q_ref.1, bf16[128,128]{1,0:T(8,128)(2,1)} %k_ref.1, bf16[128,128]{1,0:T(8,128)(2,1)} %v_ref.1, bf16[128,1024]{1,0:T(8,128)(2,1)} %o_ref.1, bf16[128,1024]{1,0:T(8,128)(2,1)} %g_ref.1, f32[8,128]{1,0:T(8,128)} %n_ref.1, s32[32,128]{1,0:T(8,128)} %bitcast.1), custom_call_target="tpu_custom_call" | custom-call | tf_op jit(solution)/shard_map/pallas_call | solution.py:574
  34.0 1.9 %shard_map.95 = (f32[128,1024]{1,0:T(8,128)}, f32[128,128]{1,0:T(8,128)}, f32[128,128]{1,0:T(8,128)}) custom-call(f32[128,1024]{1,0:T(8,128)} %get-tuple-element.5.dq_in, f32[2,128,128]{2,1,0:T(8,128)} %get-tuple-element.6.dkv_in), custom_call_target="tpu_custom_call" | custom-call | tf_op jit(solution)/shard_map/pallas_call | solution.py:587

commit v2 on v1

--- a/solution.py
+++ b/solution.py
@@ -18,19 +18,19 @@
     (),
     (STRAIGHT, STRAIGHT, ALONG, ALONG),
     (STRAIGHT, STRAIGHT, ALONG, ALONG),
-    (RELAYED, UPWARD, ALONG, UPWARD),
+    (STRAIGHT, UPWARD, ALONG, UPWARD),
 )
 SUM_ROUTE = (
     (),
-    (ALONG, STRAIGHT, ALONG, ALONG),
-    (ALONG, STRAIGHT, ALONG, ALONG),
-    (ALONG, UPWARD, ALONG, ALONG),
+    (ALONG, ALONG, ALONG, ALONG),
+    (ALONG, ALONG, ALONG, ALONG),
+    (ALONG, UPWARD, UPWARD, ALONG),
 )
 STEPS = (
-    (START, 2, 0), (START, 0, 2), (START, 1, 1), (START, 1, 0), (PASS, 2, 0), (START, 0, 3), (START, 2, 1),
-    (COMPUTE, (2, 0), (0, 0)), (PASS, 0, 2), (COMPUTE, (0, 2), (1, 0)), (PASS, 3, 0), (COMPUTE, (3, 0), (1, 1)),
-    (START, 0, 1), (PASS, 0, 3), (COMPUTE, (2, 1), (1, 2)), (COMPUTE, (2, 2), (3, 2)), (COMPUTE, (3, 1), (3, 3)),
-    (COMPUTE, (2, 3), (1, 3)), (ADD, 0, 2), (COMPUTE, (0, 1), (0, 3)), (ADD, 0, 1), (ADD, 0, 3), (ADD, 3, 0),
+    (START, 3, 0), (START, 2, 1), (START, 0, 2), (START, 2, 0), (START, 1, 1), (START, 0, 3), (PASS, 3, 0),
+    (PASS, 0, 2), (COMPUTE, (2, 1), (0, 2), (3, 0), (0, 0)), (START, 1, 0), (PASS, 0, 3), (START, 0, 1),
+    (COMPUTE, (1, 2), (2, 2), (1, 1)), (COMPUTE, (3, 2), (3, 3), (3, 1)), (COMPUTE, (2, 3), (1, 3)), (ADD, 0, 2),
+    (COMPUTE, (0, 3), (0, 1), (1, 0), (2, 0)), (ADD, 3, 0), (ADD, 0, 3), (ADD, 0, 1),
 )
 
 
@@ -369,6 +369,7 @@
 
     units = [(c, j) for c in range(planes) for j in range(layers)]
     starts = [step[1:] for step in STEPS if step[0] == START]
+    early = [step[0] for step in STEPS].index(COMPUTE)
     peers = {*starts, *(hop for unit in units for hop in key_hops(*unit)), *(sum_goes(*unit) for unit in units)}
     peers = [partner] + [at(*peer) for peer in sorted(peers - {here})]
     barrier = pltpu.get_barrier_semaphore()
@@ -388,8 +389,9 @@
 
     loads[0].wait()
     loads[1].wait()
-    for unit in starts:
-        give(here, unit)
+    for step in STEPS[:early]:
+        if step[0] == START:
+            give(here, step[1:])
 
     loads[2].wait()
     loads[3].wait()
@@ -469,8 +471,10 @@
         summed[unit] = send(out.at[unit], into.at[unit], s_send.at[unit], s_recv.at[unit], at(*sum_goes(*unit)))
 
     first = True
-    for step in STEPS:
-        if step[0] == PASS:
+    for place, step in enumerate(STEPS):
+        if step[0] == START and place > early:
+            give(here, step[1:])
+        elif step[0] == PASS:
             unit = step[1:]
             hops = key_hops(*unit)
             if hops:
@@ -503,10 +507,15 @@
         copy.wait_send()
 
 
-def finish(dq_in, dkv_in, dq_ref, dk_ref, dv_ref):
-    dq_ref[...] = dq_in[...]
-    dk_ref[...] = dkv_in[0]
-    dv_ref[...] = dkv_in[1]
+def finish(dq_in, dkv_in, dq_ref, dk_ref, dv_ref, sem):
+    copies = [
+        pltpu.make_async_copy(src, dst, sem.at[i])
+        for i, (src, dst) in enumerate(((dq_in, dq_ref), (dkv_in.at[0], dk_ref), (dkv_in.at[1], dv_ref)))
+    ]
+    for copy in copies:
+        copy.start()
+    for copy in copies:
+        copy.wait()
 
 
 def solution(mesh):
@@ -520,7 +529,7 @@
         part_rows = keys // 2
         column = layers * part_rows
         low, full = jnp.bfloat16, jnp.float32
-        vmem, hbm = pl.BlockSpec(memory_space=pltpu.VMEM), pl.BlockSpec(memory_space=pl.ANY)
+        vmem, hbm = pl.BlockSpec(memory_space=pltpu.VMEM), pl.BlockSpec(memory_space=pltpu.HBM)
         dma = pltpu.SemaphoreType.DMA
         pos = positions.reshape(-1, rows)
         if paired:
@@ -581,9 +590,11 @@
             out_specs=(vmem, vmem),
             scratch_shapes=scratch,
             compiler_params=pltpu.CompilerParams(
-                collective_id=0, has_side_effects=True, vmem_limit_bytes=58 * 2**20
+                collective_id=0, has_side_effects=True, vmem_limit_bytes=(24 if paired else 58) * 2**20
             ),
-        )(queries, key_rows, value_rows, output, out_grad, log_norm, pos)
+        )(*(pltpu.with_memory_space_constraint(x, pltpu.HBM) for x in (
+            queries, key_rows, value_rows, output, out_grad, log_norm, pos
+        )))
         return pl.pallas_call(
             finish,
             out_shape=(
@@ -592,7 +603,9 @@
                 jax.ShapeDtypeStruct((keys, width), full),
             ),
             in_specs=[vmem] * 2,
-            out_specs=(vmem, vmem, vmem),
+            out_specs=(hbm, hbm, hbm),
+            scratch_shapes=[dma((3,))],
+            compiler_params=pltpu.CompilerParams(vmem_limit_bytes=4 * 2**20),
         )(dq, dkv)
 
     return jax.shard_map(

time: 36 us -> 33.1 us (0.919)
  Pallas kernels: 35.3 us -> 32.3 us
    pallas_call x1, Pallas kernels: 33.3 us -> 31.4 us  [step(): pl.pallas_call(functools.partial(body, planes, layers), out_shape=(jax.Sh...]
    pallas_call x1, Pallas kernels: 1.9 us -> 0.85 us  [step(): pl.pallas_call(finish, out_shape=(jax.ShapeDtypeStruct((rows, columns), f...]
where the time goes in v2:
time: 33.1 us; the launch traced here: 32.9 us
  Pallas kernels  32.3 us (98%)
  between operations  0.64 us (2%)
    pallas_call x1, Pallas kernels, step(): pl.pallas_call(functools.partial(body, planes, layers), out_shape=(jax.Sh...  31.4 us
    pallas_call x1, Pallas kernels, step(): pl.pallas_call(finish, out_shape=(jax.ShapeDtypeStruct((rows, columns), f...  0.85 us

profile of v2, /device:TPU:0, one launch (start us, length us, event | category | flops | bytes accessed | tf_op | source)
XLA Modules:
  0.0 32.9 jit_solution(656646689735489268)
XLA Ops:
  0.6 31.4 %shard_map.94 = (f32[128,1024]{1,0:T(8,128)S(1)}, f32[2,128,128]{2,1,0:T(8,128)S(1)}) custom-call(bf16[128,1024]{1,0:T(8,128)(2,1)} %q_ref.1, bf16[128,128]{1,0:T(8,128)(2,1)} %k_ref.1, bf16[128,128]{1,0:T(8,128)(2,1)} %v_ref.1, bf16[128,1024]{1,0:T(8,128)(2,1)} %o_ref.1, bf16[128,1024]{1,0:T(8,128)(2,1)} %g_ref.1, f32[8,128]{1,0:T(8,128)} %n_ref.1, ...), custom_call_target="tpu_custom_call" | custom-call | tf_op jit(solution)/shard_map/pallas_call | solution.py:583
  32.1 0.9 %shard_map.95 = (f32[128,1024]{1,0:T(8,128)}, f32[128,128]{1,0:T(8,128)}, f32[128,128]{1,0:T(8,128)}) custom-call(f32[128,1024]{1,0:T(8,128)S(1)} %get-tuple-element.5.dq_in, f32[2,128,128]{2,1,0:T(8,128)S(1)} %get-tuple-element.6.dkv_in), custom_call_target="tpu_custom_call" | custom-call | tf_op jit(solution)/shard_map/pallas_call | solution.py:598

commit v3 on v2

--- a/solution.py
+++ b/solution.py
@@ -18,19 +18,19 @@
     (),
     (STRAIGHT, STRAIGHT, ALONG, ALONG),
     (STRAIGHT, STRAIGHT, ALONG, ALONG),
-    (STRAIGHT, UPWARD, ALONG, UPWARD),
+    (STRAIGHT, UPWARD, UPWARD, ALONG),
 )
 SUM_ROUTE = (
     (),
     (ALONG, ALONG, ALONG, ALONG),
     (ALONG, ALONG, ALONG, ALONG),
-    (ALONG, UPWARD, UPWARD, ALONG),
+    (ALONG, UPWARD, ALONG, UPWARD),
 )
 STEPS = (
-    (START, 3, 0), (START, 2, 1), (START, 0, 2), (START, 2, 0), (START, 1, 1), (START, 0, 3), (PASS, 3, 0),
-    (PASS, 0, 2), (COMPUTE, (2, 1), (0, 2), (3, 0), (0, 0)), (START, 1, 0), (PASS, 0, 3), (START, 0, 1),
-    (COMPUTE, (1, 2), (2, 2), (1, 1)), (COMPUTE, (3, 2), (3, 3), (3, 1)), (COMPUTE, (2, 3), (1, 3)), (ADD, 0, 2),
-    (COMPUTE, (0, 3), (0, 1), (1, 0), (2, 0)), (ADD, 3, 0), (ADD, 0, 3), (ADD, 0, 1),
+    (START, 0, 3), (START, 2, 1), (START, 0, 2), (START, 3, 0), (START, 1, 1), (PASS, 3, 0), (PASS, 0, 3),
+    (COMPUTE, (0, 3), (3, 0), (2, 1)), (START, 0, 1), (PASS, 0, 2), (START, 2, 0), (START, 1, 0),
+    (COMPUTE, (1, 3), (2, 3), (1, 1)), (COMPUTE, (3, 3), (3, 2), (3, 1)), (COMPUTE, (2, 2), (0, 1), (1, 2)),
+    (ADD, 0, 3), (ADD, 0, 1), (COMPUTE, (0, 0), (2, 0), (1, 0), (0, 2)), (ADD, 0, 2), (ADD, 3, 0),
 )
 
 

time: 33.1 us -> 32.9 us (level)
  no operation moved by 1% of the time
where the time goes in v3:
time: 32.9 us; the launch traced here: 32.7 us
  Pallas kernels  32.1 us (98%)
  between operations  0.64 us (2%)
    pallas_call x1, Pallas kernels, step(): pl.pallas_call(functools.partial(body, planes, layers), out_shape=(jax.Sh...  31.2 us
    pallas_call x1, Pallas kernels, step(): pl.pallas_call(finish, out_shape=(jax.ShapeDtypeStruct((rows, columns), f...  0.85 us

profile of v3, /device:TPU:0, one launch (start us, length us, event | category | flops | bytes accessed | tf_op | source)
XLA Modules:
  0.0 32.7 jit_solution(13280583957653060868)
XLA Ops:
  0.6 31.2 %shard_map.94 = (f32[128,1024]{1,0:T(8,128)S(1)}, f32[2,128,128]{2,1,0:T(8,128)S(1)}) custom-call(bf16[128,1024]{1,0:T(8,128)(2,1)} %q_ref.1, bf16[128,128]{1,0:T(8,128)(2,1)} %k_ref.1, bf16[128,128]{1,0:T(8,128)(2,1)} %v_ref.1, bf16[128,1024]{1,0:T(8,128)(2,1)} %o_ref.1, bf16[128,1024]{1,0:T(8,128)(2,1)} %g_ref.1, f32[8,128]{1,0:T(8,128)} %n_ref.1, ...), custom_call_target="tpu_custom_call" | custom-call | tf_op jit(solution)/shard_map/pallas_call | solution.py:583
  31.9 0.9 %shard_map.95 = (f32[128,1024]{1,0:T(8,128)}, f32[128,128]{1,0:T(8,128)}, f32[128,128]{1,0:T(8,128)}) custom-call(f32[128,1024]{1,0:T(8,128)S(1)} %get-tuple-element.5.dq_in, f32[2,128,128]{2,1,0:T(8,128)S(1)} %get-tuple-element.6.dkv_in), custom_call_target="tpu_custom_call" | custom-call | tf_op jit(solution)/shard_map/pallas_call | solution.py:598
